TPU v7x, 32 devices: a whole 2x2x4 slice. The times are simulated.
32 devices in a mesh: bond: 16 (over z, y, x), op: 2 (over core).
Axes of the slice: x: 2, y: 2, z: 4, core: 2. Of those that a mesh axis runs over, the one named last changes fastest.
Arguments:
- wavefunction: float32 [6, 256, 8192], P(None, None, 'bond'), may hold values from -6 to 6
- left_tiles: bfloat16 [16, 16, 2, 128, 128], P('op', None, None, 'bond'), may hold values from -0.375 to 0.375
- right_tiles: bfloat16 [16, 16, 2, 128, 128], P('op', None, None, 'bond'), may hold values from -0.375 to 0.375
- site_operators: float32 [16, 4, 4], P('op'), may hold values from -1.75 to 1.75
- left_charge: int32 [16], replicated, may hold values from 0 to 7, as said below
- right_charge: int32 [16], replicated, may hold values from 0 to 7, as said below
- channel_charge: int32 [16, 2], replicated, may hold values from -1 to 7, as said below
Outputs:
- sigma_one: float32 [6, 256, 8192], P(None, 'bond', 'op')
- sigma_two: float32 [6, 256, 8192], P(None, 'op', 'bond')
Inputs may be any that keep to these rules, and one draw needn't show every extreme that they name: `left_charge`: each charge labels exactly 2 of the left blocks. `right_charge`: each charge labels exactly 2 of the right blocks. `channel_charge`: column 0 is a left charge shift, each of 0 to 7 used by exactly 2 channels; column 1 is a site charge shift, each of -1, 0 and 1 used by 5 or 6 channels.
All inputs are finite; a program needn't handle non-finite values.
Results may differ from a plain program's by a relative error of at most 0.0057.
Values may be sent and summed in bfloat16 or wider, within the bound.
A program may use at most 128 MiB of HBM per device.

v0:
```python
import jax
import jax.numpy as jnp
from jax import lax
from jax.sharding import PartitionSpec as P

M = 2048
B = 128
NQ = 8
DP = 4
NB = 16
NPB = 2
site_charge_table = (0, 1, 1, 2)


def block_sources(charge, offset):
    ordering = jnp.argsort(charge, stable=True)
    target = (charge - offset) % NQ
    slot_index = target[:, None] * NPB + jnp.arange(NPB, dtype=jnp.int32)[None, :]
    return ordering[slot_index]


def site_masks(site_operators, channel_charge):
    site_charge = jnp.array(site_charge_table, dtype=jnp.int32)
    charge_step = site_charge[:, None] - site_charge[None, :]
    allowed = (charge_step[None, :, :] - channel_charge[:, 1][:, None, None]) % NQ == 0
    return jnp.where(allowed, site_operators, jnp.zeros_like(site_operators))


def pick_left(tile_full, left_order, row_class):
    slots = row_class[:, :, None] * NPB + jnp.arange(NPB, dtype=jnp.int32)[None, None, :]
    chosen = left_order[slots]

    def choose_tiles(channel_tiles, channel_rows):
        return channel_tiles[channel_rows]

    return jax.vmap(choose_tiles)(tile_full, chosen)


def right_terms(tile_piece, picked, site_matrix):
    inner_sum = jnp.einsum(
        "cjnab,ckrpjnb->ckrpja", tile_piece, picked, preferred_element_type=jnp.float32
    )
    return jnp.einsum("cpq,ckrqja->ckrpja", site_matrix, inner_sum, precision=lax.Precision.HIGHEST)


def local(
    wavefunction, left_tiles, right_tiles, site_operators, left_charge, right_charge, channel_charge
):
    bond_count = lax.axis_size("bond")
    operator_count = lax.axis_size("op")
    root_count, sector_rows, column_strip = wavefunction.shape
    local_channels = site_operators.shape[0]
    band_rows = sector_rows // bond_count
    first_channel = lax.axis_index("op") * local_channels
    own_charge = lax.dynamic_slice_in_dim(channel_charge, first_channel, local_channels, 0)
    group_width = min(column_strip, B)
    group_count = column_strip // group_width
    site_charge = jnp.array(site_charge_table, dtype=jnp.int32)
    starts = (
        lax.axis_index("bond") * column_strip
        + jnp.arange(group_count, dtype=jnp.int32) * group_width
    )
    classes = (site_charge[starts // M] + right_charge[starts % M // B]) % NQ
    left_order = jnp.argsort(left_charge, stable=True)
    first_class = (own_charge[:, 0][:, None] - classes[None, :]) % NQ
    second_class = jnp.broadcast_to((-classes % NQ)[None, :], first_class.shape)
    right_sources = jax.vmap(block_sources, in_axes=(None, 0))(
        right_charge, -(own_charge[:, 0] + own_charge[:, 1])
    )
    site_matrix = site_masks(site_operators, own_charge)
    sector_psi = wavefunction.astype(jnp.bfloat16).reshape(
        root_count, NPB, B, group_count, group_width
    )
    left_full, right_full = (
        lax.all_gather(left_tiles, "bond", axis=3, tiled=True),
        lax.all_gather(right_tiles, "bond", axis=3, tiled=True),
    )
    first_tiles = pick_left(left_full, left_order, first_class)
    left_side = jnp.einsum(
        "cgmnab,knbgw->ckmagw", first_tiles, sector_psi, preferred_element_type=jnp.float32
    )
    left_side = left_side.astype(jnp.bfloat16).reshape(
        local_channels * root_count, sector_rows, column_strip
    )
    by_rows = lax.all_to_all(left_side, "bond", split_axis=1, concat_axis=2, tiled=True)
    by_rows = by_rows.reshape(local_channels, root_count, band_rows, DP, NB, B)

    def pick_columns(channel_rows, source_index):
        return channel_rows[:, :, :, source_index]

    picked_rows = jax.vmap(pick_columns)(by_rows, right_sources)
    partial_one = right_terms(right_full, picked_rows, site_matrix).sum(axis=0)
    partial_one = partial_one.reshape(root_count, band_rows, DP * M)
    share_width = DP * M // operator_count
    summed = lax.psum(partial_one, "op")
    sigma_one = lax.dynamic_slice_in_dim(summed, lax.axis_index("op") * share_width, share_width, 2)
    rounded_one = summed.astype(jnp.bfloat16)
    rounded_blocks = rounded_one.reshape(root_count, band_rows, DP, NB, B)

    def pick_shared_columns(source_index):
        return rounded_blocks[:, :, :, source_index]

    picked_again = jax.vmap(pick_shared_columns)(right_sources)
    right_side = right_terms(right_full, picked_again, site_matrix)
    right_side = right_side.astype(jnp.bfloat16).reshape(
        local_channels * root_count, band_rows, DP * M
    )
    by_columns = lax.all_to_all(right_side, "bond", split_axis=2, concat_axis=1, tiled=True)
    by_columns = by_columns.reshape(local_channels, root_count, NPB, B, group_count, group_width)
    second_tiles = pick_left(left_full, left_order, second_class)
    partial_two = jnp.einsum(
        "cgmnab,cknbgw->ckmagw", second_tiles, by_columns, preferred_element_type=jnp.float32
    ).sum(axis=0)
    partial_two = partial_two.reshape(root_count, sector_rows, column_strip)
    sigma_two = lax.psum_scatter(partial_two, "op", scatter_dimension=1, tiled=True)
    return (sigma_one, sigma_two)


def solution(mesh):
    return jax.shard_map(
        local,
        mesh=mesh,
        in_specs=(
            P(None, None, "bond"),
            P("op", None, None, "bond", None),
            P("op", None, None, "bond", None),
            P("op", None, None),
            P(),
            P(),
            P(),
        ),
        out_specs=(P(None, "bond", "op"), P(None, "op", "bond")),
        check_vma=False,
    )
```

profile of v0, /device:TPU:0, one launch (start us, length us, event | category | flops | bytes accessed | tf_op | source)
XLA Modules:
  0.0 1423.8 jit_solution(16086372687354315001)
XLA Ops:
  7.2 0.7 all-gather.3.cloned.1.call-update
  8.0 1.3 gather_fusion
  9.3 1.3 gather_fusion.1
  10.6 0.5 fusion.47
  11.3 0.1 reshape.438
  11.4 1.9 sort.34
  13.4 0.8 gather_fusion.2
  14.1 0.1 gather.36
  14.3 0.1 reshape.468
  14.4 2.1 convert_element_type.18
  16.5 0.4 reshape.412
  16.9 138.4 %all-gather.3.cloned.1.call-done = bf16[8,16,2,128,128]{4,3,2,1,0:T(8,128)(2,1)} async-done(((bf16[8,16,2,8,128]{4,3,2,1,0:T(8,128)(2,1)}), bf16[8,16,2,128,128]{4,3,2,1,0:T(8,128)(2,1)}) %all-gather.3.cloned.1.call-update) | async-done | bytes 8388624 | tf_op jit(solution)/shard_map/all_gather | solution.py:75
  155.3 6.4 gather_fusion.6
  161.7 6.9 fusion.10
  168.6 32.3 %copy.103 = bf16[8,6,2,128,4,128]{5,4,1,0,3,2:T(4,128)(2,1)} copy(bf16[8,6,2,128,4,128]{5,3,1,2,0,4:T(8,128)(2,1)S(1)} %fusion.10) | data formatting | bytes 25165824 | tf_op jit(solution)/shard_map/reshape | solution.py:82
  201.0 19.0 %reshape.505 = bf16[48,256,512]{2,0,1:T(8,128)(2,1)} reshape(bf16[8,6,2,128,4,128]{5,4,1,0,3,2:T(4,128)(2,1)} %copy.103) | data formatting | bytes 25165824 | tf_op jit(solution)/shard_map/reshape | solution.py:82
  220.0 5.1 all-to-all-start
  225.1 0.7 all-gather.5.cloned.1.call-update
  225.8 0.2 all-reduce.2.cloned.1.call-start
  226.0 1.2 sort.35
  227.4 0.1 compare_select_fusion.1
  227.5 0.1 reshape.446
  227.6 1.9 gather_fusion.3
  229.5 0.1 gather.39
  229.7 0.1 reshape.474
  229.9 0.1 select_bitcast_fusion
  230.0 272.9 %all-to-all-done = bf16[48,256,512]{2,0,1:T(8,128)(2,1)} async-done(((bf16[48,256,512]{2,0,1:T(8,128)(2,1)}), bf16[48,256,512]{2,0,1:T(8,128)(2,1)}, u32[]{:S(2)}, u32[]{:S(2)}) %all-to-all-start) | async-done | bytes 12582944 | tf_op jit(solution)/shard_map/all_to_all | solution.py:85
  502.9 14.4 %copy.149 = bf16[48,16,16,512]{3,1,2,0:T(8,128)(2,1)} copy(bf16[48,16,16,512]{3,0,2,1:T(8,128)(2,1)} %bitcast.9) | data formatting | bytes 25165824 | tf_op jit(solution)/shard_map/all_to_all | solution.py:85
  517.4 20.3 %reshape.414 = bf16[8,6,16,4,16,128]{5,4,3,2,1,0:T(8,128)(2,1)} reshape(bf16[48,16,16,512]{3,2,1,0:T(8,128)(2,1)} %bitcast.117) | data formatting | bytes 25165824 | tf_op jit(solution)/shard_map/reshape | solution.py:86
  537.6 25.7 %copy.72 = bf16[8,6,16,4,16,128]{5,2,4,3,1,0:T(8,128)(2,1)} copy(bf16[8,6,16,4,16,128]{5,4,3,2,1,0:T(8,128)(2,1)} %reshape.414) | data formatting | bytes 25165824 | tf_op jit(solution)/shard_map/reshape | solution.py:86
  563.4 19.4 %gather_fusion.7 = bf16[256,6,16,4,128]{4,2,3,1,0:T(8,128)(2,1)} fusion(bf16[8,6,16,4,16,128]{5,2,4,3,1,0:T(8,128)(2,1)} %copy.72, s32[256]{0:T(256)S(1)} %reshape.474), kind=kCustom, calls=%fused_computation.7 | custom fusion | bytes 50333696 | tf_op jit(solution)/shard_map/vmap()/gather | solution.py:89
  582.8 6.0 all-gather.5.cloned.1.call-done
  588.7 23.5 %fusion.15 = f32[8,6,16,4,16,128]{5,2,3,1,4,0:T(8,128)} fusion(bf16[8,16,2,6,16,4,128]{6,4,5,3,2,1,0:T(8,128)(2,1)} %bitcast.115, bf16[8,16,2,128,128]{4,3,2,1,0:T(8,128)(2,1)} %all-gather.5.cloned.1.call-done), kind=kOutput, calls=%fused_computation.25 | convolution fusion | flops 3221225472 | bytes 58720256 | tf_op jit(solution)/shard_map/cjnab,ckrpjnb->ckrpja/dot_general | solution.py:40
  612.3 32.9 %fusion.25 = f32[6,16,4,16,128]{4,2,3,1,0:T(4,128)S(1)} fusion(f32[8,6,16,4,16,128]{5,2,3,1,4,0:T(8,128)} %fusion.15, f32[8,4,4,1,1,1]{0,2,1,5,4,3:T(4,128)S(1)} %select_bitcast_fusion), kind=kOutput, calls=%fused_computation.31 | convolution fusion | flops 301989888 | bytes 28312064 | tf_op jit(solution)/shard_map/cpq,ckrqja->ckrpja/dot_general | solution.py:43
  645.2 0.3 copy.76
  645.5 2.4 reshape.415
  647.9 0.1 copy.95
  648.0 0.1 reshape.454
  648.2 131.5 %all-reduce.2.cloned.1.call-done = f32[6,16,8192]{2,1,0:T(8,128)} async-done(((f32[6,16,8192]{2,1,0:T(8,128)}), f32[6,16,8192]{2,1,0:T(8,128)}) %all-reduce.2.cloned.1.call-update) | async-done | bytes 3145744 | tf_op jit(solution)/shard_map/psum | solution.py:95
  779.7 2.1 convert_element_type.21
  781.8 0.4 copy.113
  782.2 1.0 copy.77
  783.2 13.6 gather_fusion.4
  796.8 23.5 %fusion.18 = f32[8,6,16,4,16,128]{5,2,3,1,4,0:T(8,128)} fusion(bf16[8,16,2,6,16,4,128]{6,4,5,3,2,1,0:T(8,128)(2,1)} %bitcast.116, bf16[8,16,2,128,128]{4,3,2,1,0:T(8,128)(2,1)} %all-gather.5.cloned.1.call-done), kind=kOutput, calls=%fused_computation.26 | convolution fusion | flops 3221225472 | bytes 58720256 | tf_op jit(solution)/shard_map/cjnab,ckrpjnb->ckrpja/dot_general | solution.py:40
  820.4 56.9 %convert_bitcast_fusion = bf16[8,6,16,4,16,128]{5,3,4,2,1,0:T(4,128)(2,1)S(1)} fusion(f32[8,4,4,1,1,1]{2,1,5,4,3,0:T(4,128)S(1)} %copy.95, f32[8,6,16,4,16,128]{5,2,3,1,4,0:T(8,128)} %fusion.18), kind=kOutput, calls=%fused_computation.24 | convolution fusion | flops 308281344 | bytes 37749248 | tf_op jit(solution)/shard_map/cpq,ckrqja->ckrpja/dot_general | solution.py:43
  877.3 6.5 copy.81
  883.8 19.3 %reshape.417 = bf16[48,16,8192]{2,1,0:T(8,128)(2,1)} reshape(bf16[8,6,16,4,16,128]{5,4,3,2,1,0:T(8,128)(2,1)} %copy.81) | data formatting | bytes 25165824 | tf_op jit(solution)/shard_map/reshape | solution.py:105
  903.1 47.8 %copy.82 = bf16[48,16,8192]{0,1,2:T(8,128)(2,1)} copy(bf16[48,16,8192]{2,1,0:T(8,128)(2,1)} %reshape.417) | data formatting | bytes 25165824 | tf_op jit(solution)/shard_map/reshape | solution.py:105
  950.9 51.9 %reshape.506 = bf16[16,2,196608]{2,1,0:T(2,128)(2,1)} reshape(bf16[8192,16,48]{2,1,0:T(8,128)(2,1)} %bitcast.113) | data formatting | bytes 25165824
  1002.8 7.0 all-to-all-start.1
  1009.9 0.1 reshape.462
  1010.1 0.8 gather_fusion.5
  1010.8 0.1 gather.43
  1011.0 0.1 reshape.480
  1011.1 6.5 gather_fusion.8
  1017.6 229.6 %all-to-all-done.1 = bf16[16,2,196608]{2,1,0:T(2,128)(2,1)} async-done(((bf16[16,2,196608]{2,1,0:T(2,128)(2,1)}), bf16[16,2,196608]{2,1,0:T(2,128)(2,1)}, u32[]{:S(2)}, u32[]{:S(2)}) %all-to-all-start.1) | async-done | bytes 12582944 | tf_op jit(solution)/shard_map/all_to_all | solution.py:108
  1247.2 33.6 %reshape.507 = bf16[8192,16,48]{2,1,0:T(8,128)(2,1)} reshape(bf16[16,2,196608]{2,1,0:T(2,128)(2,1)} %all-to-all-done.1) | data formatting | bytes 25165824
  1280.8 40.1 %copy.83 = bf16[48,16,16,512]{3,1,2,0:T(8,128)(2,1)} copy(bf16[48,16,16,512]{0,1,3,2:T(8,128)(2,1)} %bitcast.114) | data formatting | bytes 25165824 | tf_op jit(solution)/shard_map/all_to_all | solution.py:108
  1320.8 18.2 %reshape.418 = bf16[8,6,2,128,4,128]{5,4,3,2,1,0:T(4,128)(2,1)} reshape(bf16[48,16,16,512]{3,2,1,0:T(8,128)(2,1)} %bitcast.118) | data formatting | bytes 25165824 | tf_op jit(solution)/shard_map/reshape | solution.py:109
  1339.0 11.7 fusion.28
  1350.7 3.3 copy.86
  1353.9 2.8 reshape.419
  1356.8 2.7 constant_dynamic-slice_fusion
  1359.4 57.6 %reduce-scatter.2.cloned.1.call-done = f32[6,128,512]{2,1,0:T(8,128)} async-done(((f32[6,256,512]{2,1,0:T(8,128)}), f32[6,128,512]{2,1,0:T(8,128)}) %reduce-scatter.2.cloned.1.call-update) | async-done | bytes 1572880 | tf_op jit(solution)/shard_map/reduce_scatter | solution.py:115
  (42 shorter events, 0.8 us)
Async XLA Ops:
  7.2 3.4 copy-start
  7.2 148.1 %all-gather.3.cloned.1.call-start = ((), (), s32[]{:S(2)}) async-start(), calls=%async_computation.3 | async-start | bytes 8912896 | tf_op jit(solution)/shard_map/all_gather | solution.py:75
  13.3 148.3 %copy-start.2 = (s32[16]{0:T(128)}, s32[16]{0:T(128)S(1)}, u32[]{:S(2)}) copy-start(s32[16]{0:T(128)S(1)} %get-tuple-element.4) | copy-start | bytes 196
  220.0 6.1 copy-start.4
  220.0 282.9 %all-to-all-start = ((bf16[48,256,512]{2,0,1:T(8,128)(2,1)}), bf16[48,256,512]{2,0,1:T(8,128)(2,1)}, u32[]{:S(2)}, u32[]{:S(2)}) async-start(bf16[48,256,512]{2,0,1:T(8,128)(2,1)} %reshape.505), calls=%async_computation | async-start | bytes 25165824 | tf_op jit(solution)/shard_map/all_to_all | solution.py:85
  225.0 363.7 %all-gather.5.cloned.1.call-start = ((), (), s32[]{:S(2)}) async-start(), calls=%async_computation.4 | async-start | bytes 8912896 | tf_op jit(solution)/shard_map/all_gather | solution.py:76
  225.8 553.9 %all-reduce.2.cloned.1.call-start = ((), (), s32[]{:S(2)}) async-start(), calls=%async_computation.5 | async-start | bytes 6291456 | tf_op jit(solution)/shard_map/psum | solution.py:95
  227.6 2.2 copy-start.5
  227.6 2.2 copy-start.8
  227.6 2.3 copy-start.6
  1002.8 7.0 copy-start.7
  1002.8 7.3 copy-start.3
  1002.8 244.3 %all-to-all-start.1 = ((bf16[16,2,196608]{2,1,0:T(2,128)(2,1)}), bf16[16,2,196608]{2,1,0:T(2,128)(2,1)}, u32[]{:S(2)}, u32[]{:S(2)}) async-start(bf16[16,2,196608]{2,1,0:T(2,128)(2,1)} %reshape.506), calls=%async_computation.1 | async-start | bytes 25165824 | tf_op jit(solution)/shard_map/all_to_all | solution.py:108
  1009.8 407.3 %reduce-scatter.2.cloned.1.call-start = ((), (), s32[]{:S(2)}) async-start(), calls=%async_computation.6 | async-start | bytes 4718592 | tf_op jit(solution)/shard_map/reduce_scatter | solution.py:115
  1339.0 78.1 %copy-start.1 = (s32[16,2]{0,1:T(2,128)S(1)}, s32[16,2]{0,1:T(2,128)}, u32[]{:S(2)}) copy-start(s32[16,2]{0,1:T(2,128)} %param.15) | copy-start | bytes 388
Sparse Core Ops, SparseCore 0:
  10.7 144.5 all-gather.2
  228.6 360.1 all-gather.4
  648.1 131.6 all-reduce.1
  1356.9 60.1 reduce-scatter.1
where the time goes:
time: 1430 us; the launch traced here: 1420 us
  waiting for transfers between devices  837 us (59%)
  local copies, waits for them, and re-layouts  396 us (28%)
  matrix products  156 us (11%)
  between operations  14.3 us (1%)
    all_to_all x1, waiting for transfers between devices, local(): lax.all_to_all(left_side, 'bond', split_axis=1, concat_axis=2, tiled=True)  273 us
    all_to_all x1, waiting for transfers between devices, local(): lax.all_to_all(right_side, 'bond', split_axis=2, concat_axis=1, tiled=True)  230 us
    all_gather x1, waiting for transfers between devices, local(): lax.all_gather(left_tiles, 'bond', axis=3, tiled=True)  138 us
    psum x1, waiting for transfers between devices, local(): summed = lax.psum(partial_one, 'op')  132 us
    dot_general x2, matrix products, right_terms(): jnp.einsum('cpq,ckrqja->ckrpja', site_matrix, inner_sum, precision=lax.Pr...  89.8 us
    unnamed x21, local copies, waits for them, and re-layouts  86 us
    reshape x2, local copies, waits for them, and re-layouts, local(): right_side.astype(jnp.bfloat16)  67 us
    reduce_scatter x1, waiting for transfers between devices, local(): lax.psum_scatter(partial_two, 'op', scatter_dimension=1, tiled=True)  57.6 us
  transfers between devices with their start and end apart: 6, of which 6 were waited for; matrix products, arithmetic and copies ran while one was open for 7% of the time, Pallas kernels for 0%

commit v1 on v0

--- a/solution.py
+++ b/solution.py
@@ -1,3 +1,4 @@
+import functools
 import jax
 import jax.numpy as jnp
 from jax import lax
@@ -10,6 +11,23 @@
 NB = 16
 NPB = 2
 site_charge_table = (0, 1, 1, 2)
+
+
+def lead_things(matrix, pos_dim):
+    raw_out, spare = (lax.axis_size("bond"), lax.axis_index("bond"))
+    f_now, z = (matrix, 1)
+    while z < raw_out:
+        f_next = lax.ppermute(
+            f_now, axis_name="bond", perm=[(to_i, to_i ^ z) for to_i in range(raw_out)]
+        )
+        heard = jnp.concatenate([f_now, f_next], axis=pos_dim)
+        q_next = jnp.concatenate([f_next, f_now], axis=pos_dim)
+        f_now = jnp.where(spare & z == 0, heard, q_next)
+        z = 2 * z
+    return f_now
+
+
+put_array_up = functools.partial(lead_things, pos_dim=3)
 
 
 def block_sources(charge, offset):
@@ -72,7 +90,7 @@
         root_count, NPB, B, group_count, group_width
     )
     left_full, right_full = (
-        lax.all_gather(left_tiles, "bond", axis=3, tiled=True),
+        put_array_up(left_tiles),
         lax.all_gather(right_tiles, "bond", axis=3, tiled=True),
     )
     first_tiles = pick_left(left_full, left_order, first_class)

time: 1430 us -> 1570 us (1.098)
  waiting for transfers between devices: 837 us -> 947 us
  other arithmetic: 8.51 us -> 28.4 us
    ppermute x0 -> x4, waiting for transfers between devices: none -> 251 us  [lead_things(): lax.ppermute(f_now, axis_name='bond', perm=[(to_i, to_i ^ z) for to_i in...]
    all_gather x1 -> x0, waiting for transfers between devices: 138 us -> none  [local(): lax.all_gather(left_tiles, 'bond', axis=3, tiled=True)]
    select_n x0 -> x4, other arithmetic: none -> 20.6 us  [lead_things(): f_now = jnp.where(spare & z == 0, heard, q_next)]
    unnamed x21 -> x23, local copies, waits for them, and re-layouts: 86 us -> 86 us
  transfers between devices with their start and end apart: 6 -> 9, of which waited for: 6 -> 8; matrix products, arithmetic and copies ran while one was open for 7% -> 6% of each run, Pallas kernels for 0% -> 0%
where the time goes in v1:
time: 1570 us; the launch traced here: 1560 us
  waiting for transfers between devices  947 us (60%)
  local copies, waits for them, and re-layouts  394 us (25%)
  matrix products  156 us (10%)
  other arithmetic  28.4 us (2%)
  starting transfers between devices  22.5 us (1%)
    all_to_all x1, waiting for transfers between devices, local(): lax.all_to_all(left_side, 'bond', split_axis=1, concat_axis=2, tiled=True)  283 us
    ppermute x4, waiting for transfers between devices, lead_things(): lax.ppermute(f_now, axis_name='bond', perm=[(to_i, to_i ^ z) for to_i in...  251 us
    all_to_all x1, waiting for transfers between devices, local(): lax.all_to_all(right_side, 'bond', split_axis=2, concat_axis=1, tiled=True)  230 us
    psum x1, waiting for transfers between devices, local(): summed = lax.psum(partial_one, 'op')  125 us
    dot_general x2, matrix products, right_terms(): jnp.einsum('cpq,ckrqja->ckrpja', site_matrix, inner_sum, precision=lax.Pr...  89.8 us
    unnamed x23, local copies, waits for them, and re-layouts  86 us
    reshape x2, local copies, waits for them, and re-layouts, local(): right_side.astype(jnp.bfloat16)  67 us
    reduce_scatter x1, waiting for transfers between devices, local(): lax.psum_scatter(partial_two, 'op', scatter_dimension=1, tiled=True)  57.6 us
  transfers between devices with their start and end apart: 9, of which 8 were waited for; matrix products, arithmetic and copies ran while one was open for 6% of the time, Pallas kernels for 0%

profile of v1, /device:TPU:0, one launch (start us, length us, event | category | flops | bytes accessed | tf_op | source)
XLA Modules:
  0.0 1561.8 jit_solution(17237081784284908915)
XLA Ops:
  7.2 3.0 collective-permute-start
  10.2 12.1 collective-permute-done
  22.4 1.6 maximum_select_fusion.3
  24.0 1.8 collective-permute-start.1
  25.8 22.7 %collective-permute-done.1 = bf16[8,16,2,16,128]{4,3,2,1,0:T(8,128)(2,1)} collective-permute-done((bf16[8,16,2,16,128]{4,3,2,1,0:T(8,128)(2,1)S(1)}, bf16[8,16,2,16,128]{4,3,2,1,0:T(8,128)(2,1)}, u32[]{:S(2)}, u32[]{:S(2)}) %collective-permute-start.1) | collective-permute-done | bytes 1048608 | tf_op jit(solution)/shard_map/ppermute | solution.py:20
  48.5 2.3 maximum_select_fusion.2
  50.8 1.6 collective-permute-start.2
  52.4 44.5 %collective-permute-done.2 = bf16[8,16,2,32,128]{4,3,2,1,0:T(8,128)(2,1)} collective-permute-done((bf16[8,16,2,32,128]{4,3,2,1,0:T(8,128)(2,1)S(1)}, bf16[8,16,2,32,128]{4,3,2,1,0:T(8,128)(2,1)}, u32[]{:S(2)}, u32[]{:S(2)}) %collective-permute-start.2) | collective-permute-done | bytes 2097184 | tf_op jit(solution)/shard_map/ppermute | solution.py:20
  96.9 5.0 maximum_select_fusion.1
  101.9 2.3 collective-permute-start.3
  104.2 0.6 gather_fusion
  104.9 0.6 gather_fusion.1
  105.6 0.5 fusion.47
  106.4 1.2 sort.34
  107.7 0.8 gather_fusion.2
  108.7 2.1 convert_element_type.18
  110.8 0.4 reshape.412
  111.3 171.8 %collective-permute-done.3 = bf16[8,16,2,64,128]{4,3,2,1,0:T(8,128)(2,1)} collective-permute-done((bf16[8,16,2,64,128]{4,3,2,1,0:T(8,128)(2,1)}, bf16[8,16,2,64,128]{4,3,2,1,0:T(8,128)(2,1)}, u32[]{:S(2)}, u32[]{:S(2)}) %collective-permute-start.3) | collective-permute-done | bytes 4194336 | tf_op jit(solution)/shard_map/ppermute | solution.py:20
  283.0 11.7 maximum_select_fusion
  294.7 6.4 gather_fusion.6
  301.1 6.9 fusion.10
  308.1 32.2 %copy.103 = bf16[8,6,2,128,4,128]{5,4,1,0,3,2:T(4,128)(2,1)} copy(bf16[8,6,2,128,4,128]{5,3,1,2,0,4:T(8,128)(2,1)S(1)} %fusion.10) | data formatting | bytes 25165824 | tf_op jit(solution)/shard_map/reshape | solution.py:100
  340.3 19.0 %reshape.505 = bf16[48,256,512]{2,0,1:T(8,128)(2,1)} reshape(bf16[8,6,2,128,4,128]{5,4,1,0,3,2:T(4,128)(2,1)} %copy.103) | data formatting | bytes 25165824 | tf_op jit(solution)/shard_map/reshape | solution.py:100
  359.3 6.2 all-to-all-start
  365.6 0.7 all-gather.2.cloned.1.call-update
  366.3 0.5 all-reduce.2.cloned.1.call-start
  366.8 1.2 sort.35
  368.2 0.1 reshape.446
  368.4 1.9 gather_fusion.3
  370.3 0.1 gather.39
  370.4 0.1 reshape.474
  370.7 282.5 %all-to-all-done = bf16[48,256,512]{2,0,1:T(8,128)(2,1)} async-done(((bf16[48,256,512]{2,0,1:T(8,128)(2,1)}), bf16[48,256,512]{2,0,1:T(8,128)(2,1)}, u32[]{:S(2)}, u32[]{:S(2)}) %all-to-all-start) | async-done | bytes 12582944 | tf_op jit(solution)/shard_map/all_to_all | solution.py:103
  653.3 14.4 copy.149
  667.7 20.3 %reshape.414 = bf16[8,6,16,4,16,128]{5,4,3,2,1,0:T(8,128)(2,1)} reshape(bf16[48,16,16,512]{3,2,1,0:T(8,128)(2,1)} %bitcast.117) | data formatting | bytes 25165824 | tf_op jit(solution)/shard_map/reshape | solution.py:104
  688.0 25.7 %copy.72 = bf16[8,6,16,4,16,128]{5,2,4,3,1,0:T(8,128)(2,1)} copy(bf16[8,6,16,4,16,128]{5,4,3,2,1,0:T(8,128)(2,1)} %reshape.414) | data formatting | bytes 25165824 | tf_op jit(solution)/shard_map/reshape | solution.py:104
  713.7 19.3 %gather_fusion.7 = bf16[256,6,16,4,128]{4,2,3,1,0:T(8,128)(2,1)} fusion(bf16[8,6,16,4,16,128]{5,2,4,3,1,0:T(8,128)(2,1)} %copy.72, s32[256]{0:T(256)S(1)} %reshape.474), kind=kCustom, calls=%fused_computation.7 | custom fusion | bytes 50333696 | tf_op jit(solution)/shard_map/vmap()/gather | solution.py:107
  733.1 23.5 %fusion.15 = f32[8,6,16,4,16,128]{5,2,3,1,4,0:T(8,128)} fusion(bf16[8,16,2,6,16,4,128]{6,4,5,3,2,1,0:T(8,128)(2,1)} %bitcast.115, bf16[8,16,2,128,128]{4,3,2,1,0:T(8,128)(2,1)} %all-gather.2.cloned.1.call-done), kind=kOutput, calls=%fused_computation.25 | convolution fusion | flops 3221225472 | bytes 58720256 | tf_op jit(solution)/shard_map/cjnab,ckrpjnb->ckrpja/dot_general | solution.py:58
  756.6 32.7 %fusion.25 = f32[6,16,4,16,128]{4,2,3,1,0:T(4,128)S(1)} fusion(f32[8,6,16,4,16,128]{5,2,3,1,4,0:T(8,128)} %fusion.15, f32[8,4,4,1,1,1]{0,2,1,5,4,3:T(4,128)S(1)} %select_bitcast_fusion), kind=kOutput, calls=%fused_computation.34 | convolution fusion | flops 301989888 | bytes 28312064 | tf_op jit(solution)/shard_map/cpq,ckrqja->ckrpja/dot_general | solution.py:61
  789.3 0.3 copy.76
  789.6 2.4 reshape.415
  792.1 0.1 reshape.454
  792.3 125.3 %all-reduce.2.cloned.1.call-done = f32[6,16,8192]{2,1,0:T(8,128)} async-done(((f32[6,16,8192]{2,1,0:T(8,128)}), f32[6,16,8192]{2,1,0:T(8,128)}) %all-reduce.2.cloned.1.call-update) | async-done | bytes 3145744 | tf_op jit(solution)/shard_map/psum | solution.py:113
  917.6 2.1 convert_element_type.21
  919.6 0.4 copy.113
  920.1 1.0 copy.77
  921.1 13.6 gather_fusion.4
  934.7 23.5 %fusion.18 = f32[8,6,16,4,16,128]{5,2,3,1,4,0:T(8,128)} fusion(bf16[8,16,2,6,16,4,128]{6,4,5,3,2,1,0:T(8,128)(2,1)} %bitcast.116, bf16[8,16,2,128,128]{4,3,2,1,0:T(8,128)(2,1)} %all-gather.2.cloned.1.call-done), kind=kOutput, calls=%fused_computation.26 | convolution fusion | flops 3221225472 | bytes 58720256 | tf_op jit(solution)/shard_map/cjnab,ckrpjnb->ckrpja/dot_general | solution.py:58
  958.2 57.2 %convert_bitcast_fusion = bf16[8,6,16,4,16,128]{5,3,4,2,1,0:T(4,128)(2,1)S(1)} fusion(f32[8,4,4,1,1,1]{2,1,5,4,3,0:T(4,128)S(1)} %copy.95, f32[8,6,16,4,16,128]{5,2,3,1,4,0:T(8,128)} %fusion.18), kind=kOutput, calls=%fused_computation.24 | convolution fusion | flops 308281344 | bytes 37749248 | tf_op jit(solution)/shard_map/cpq,ckrqja->ckrpja/dot_general | solution.py:61
  1015.4 6.5 copy.81
  1021.9 19.3 %reshape.417 = bf16[48,16,8192]{2,1,0:T(8,128)(2,1)} reshape(bf16[8,6,16,4,16,128]{5,4,3,2,1,0:T(8,128)(2,1)} %copy.81) | data formatting | bytes 25165824 | tf_op jit(solution)/shard_map/reshape | solution.py:123
  1041.2 47.8 %copy.82 = bf16[48,16,8192]{0,1,2:T(8,128)(2,1)} copy(bf16[48,16,8192]{2,1,0:T(8,128)(2,1)} %reshape.417) | data formatting | bytes 25165824 | tf_op jit(solution)/shard_map/reshape | solution.py:123
  1088.9 51.9 %reshape.506 = bf16[16,2,196608]{2,1,0:T(2,128)(2,1)} reshape(bf16[8192,16,48]{2,1,0:T(8,128)(2,1)} %bitcast.113) | data formatting | bytes 25165824
  1140.8 7.0 all-to-all-start.1
  1148.1 0.8 gather_fusion.5
  1149.1 6.5 gather_fusion.8
  1155.6 229.6 %all-to-all-done.1 = bf16[16,2,196608]{2,1,0:T(2,128)(2,1)} async-done(((bf16[16,2,196608]{2,1,0:T(2,128)(2,1)}), bf16[16,2,196608]{2,1,0:T(2,128)(2,1)}, u32[]{:S(2)}, u32[]{:S(2)}) %all-to-all-start.1) | async-done | bytes 12582944 | tf_op jit(solution)/shard_map/all_to_all | solution.py:126
  1385.2 33.6 %reshape.507 = bf16[8192,16,48]{2,1,0:T(8,128)(2,1)} reshape(bf16[16,2,196608]{2,1,0:T(2,128)(2,1)} %all-to-all-done.1) | data formatting | bytes 25165824
  1418.8 40.1 %copy.83 = bf16[48,16,16,512]{3,1,2,0:T(8,128)(2,1)} copy(bf16[48,16,16,512]{0,1,3,2:T(8,128)(2,1)} %bitcast.114) | data formatting | bytes 25165824 | tf_op jit(solution)/shard_map/all_to_all | solution.py:126
  1458.9 18.2 %reshape.418 = bf16[8,6,2,128,4,128]{5,4,3,2,1,0:T(4,128)(2,1)} reshape(bf16[48,16,16,512]{3,2,1,0:T(8,128)(2,1)} %bitcast.118) | data formatting | bytes 25165824 | tf_op jit(solution)/shard_map/reshape | solution.py:127
  1477.0 11.7 fusion.28
  1488.7 3.3 copy.86
  1492.0 2.8 reshape.419
  1494.8 2.7 constant_dynamic-slice_fusion
  1497.5 57.6 %reduce-scatter.2.cloned.1.call-done = f32[6,128,512]{2,1,0:T(8,128)} async-done(((f32[6,256,512]{2,1,0:T(8,128)}), f32[6,128,512]{2,1,0:T(8,128)}) %reduce-scatter.2.cloned.1.call-update) | async-done | bytes 1572880 | tf_op jit(solution)/shard_map/reduce_scatter | solution.py:133
  (53 shorter events, 1.7 us)
Async XLA Ops:
  7.2 98.4 %copy-start = (s32[16,2]{0,1:T(2,128)S(1)}, s32[16,2]{0,1:T(2,128)}, u32[]{:S(2)}) copy-start(s32[16,2]{0,1:T(2,128)} %param.15) | copy-start | bytes 388
  7.2 97.1 %copy-start.5 = (s32[4]{0:T(128)S(1)}, s32[4]{0:T(128)}, u32[]{:S(2)}) copy-start(s32[4]{0:T(128)} %constant.119.clone) | copy-start | bytes 52
  7.2 97.7 %copy-start.4 = (s32[16]{0:T(128)S(1)}, s32[16]{0:T(128)}, u32[]{:S(2)}) copy-start(s32[16]{0:T(128)} %param.14) | copy-start | bytes 196
  7.2 99.2 %copy-start.9 = (s32[16]{0:T(128)S(1)}, s32[16]{0:T(128)}, u32[]{:S(2)}) copy-start(s32[16]{0:T(128)} %param.13) | copy-start | bytes 196
  7.2 15.2 collective-permute-start
  24.0 24.5 %collective-permute-start.1 = (bf16[8,16,2,16,128]{4,3,2,1,0:T(8,128)(2,1)S(1)}, bf16[8,16,2,16,128]{4,3,2,1,0:T(8,128)(2,1)}, u32[]{:S(2)}, u32[]{:S(2)}) collective-permute-start(bf16[8,16,2,16,128]{4,3,2,1,0:T(8,128)(2,1)S(1)} %maximum_select_fusion.3), channel_id=1, source_target_pairs={{0,4},{2,6},{4,0},{6,2},{8,12},{10,14},{12,8},{14,10},{16,20},{18,... | collective-permute-start | bytes 3145736 | tf_op jit(solution)/shard_map/ppermute | solution.py:20
  50.8 46.1 %collective-permute-start.2 = (bf16[8,16,2,32,128]{4,3,2,1,0:T(8,128)(2,1)S(1)}, bf16[8,16,2,32,128]{4,3,2,1,0:T(8,128)(2,1)}, u32[]{:S(2)}, u32[]{:S(2)}) collective-permute-start(bf16[8,16,2,32,128]{4,3,2,1,0:T(8,128)(2,1)S(1)} %maximum_select_fusion.2), channel_id=1, source_target_pairs={{0,8},{2,10},{4,12},{6,14},{8,0},{10,2},{12,4},{14,6},{16,24},{18,... | collective-permute-start | bytes 6291464 | tf_op jit(solution)/shard_map/ppermute | solution.py:20
  101.9 181.1 %collective-permute-start.3 = (bf16[8,16,2,64,128]{4,3,2,1,0:T(8,128)(2,1)}, bf16[8,16,2,64,128]{4,3,2,1,0:T(8,128)(2,1)}, u32[]{:S(2)}, u32[]{:S(2)}) collective-permute-start(bf16[8,16,2,64,128]{4,3,2,1,0:T(8,128)(2,1)} %maximum_select_fusion.1), channel_id=1, source_target_pairs={{0,16},{2,18},{4,20},{6,22},{8,24},{10,26},{12,28},{14,30},{16,0},... | collective-permute-start | bytes 12582920 | tf_op jit(solution)/shard_map/ppermute | solution.py:20
  107.7 0.8 copy-start.2
  359.3 293.9 %all-to-all-start = ((bf16[48,256,512]{2,0,1:T(8,128)(2,1)}), bf16[48,256,512]{2,0,1:T(8,128)(2,1)}, u32[]{:S(2)}, u32[]{:S(2)}) async-start(bf16[48,256,512]{2,0,1:T(8,128)(2,1)} %reshape.505), calls=%async_computation | async-start | bytes 25165824 | tf_op jit(solution)/shard_map/all_to_all | solution.py:103
  365.5 367.5 %all-gather.2.cloned.1.call-start = ((), (), s32[]{:S(2)}) async-start(), calls=%async_computation.3 | async-start | bytes 8912896 | tf_op jit(solution)/shard_map/all_gather | solution.py:94
  366.3 551.3 %all-reduce.2.cloned.1.call-start = ((), (), s32[]{:S(2)}) async-start(), calls=%async_computation.4 | async-start | bytes 6291456 | tf_op jit(solution)/shard_map/psum | solution.py:113
  368.4 2.2 copy-start.8
  368.4 2.3 copy-start.6
  1140.8 7.0 copy-start.7
  1140.8 7.2 copy-start.3
  1140.8 244.3 %all-to-all-start.1 = ((bf16[16,2,196608]{2,1,0:T(2,128)(2,1)}), bf16[16,2,196608]{2,1,0:T(2,128)(2,1)}, u32[]{:S(2)}, u32[]{:S(2)}) async-start(bf16[16,2,196608]{2,1,0:T(2,128)(2,1)} %reshape.506), calls=%async_computation.1 | async-start | bytes 25165824 | tf_op jit(solution)/shard_map/all_to_all | solution.py:126
  1147.8 407.3 %reduce-scatter.2.cloned.1.call-start = ((), (), s32[]{:S(2)}) async-start(), calls=%async_computation.5 | async-start | bytes 4718592 | tf_op jit(solution)/shard_map/reduce_scatter | solution.py:133
  1477.0 78.0 %copy-start.1 = (s32[16,2]{0,1:T(2,128)S(1)}, s32[16,2]{0,1:T(2,128)}, u32[]{:S(2)}) copy-start(s32[16,2]{0,1:T(2,128)} %param.15) | copy-start | bytes 388
Sparse Core Ops, SparseCore 0:
  369.1 359.4 all-gather.1
  792.1 125.3 all-reduce.1
  1494.9 60.1 reduce-scatter.1
